TPU v7x, 32 devices: a whole 2x2x4 slice. The times are simulated.
32 devices in a mesh: wide: 16 (over z, x, core), narrow: 2 (over y).
Axes of the slice: x: 2, y: 2, z: 4, core: 2. Of those that a mesh axis runs over, the one named last changes fastest.
Arguments:
- tokens: bfloat16 [65536, 384], P(('wide', 'narrow')), may hold values from -6 to 6
- counts: int32 [1024], P(('wide', 'narrow')), may hold values from 13 to 64, as said below
- cotangent: bfloat16 [65536, 384], P(('wide', 'narrow')), may hold values from -6 to 6
- master: float32 [1773312], P(('wide', 'narrow'))
- first: float32 [1773312], P(('wide', 'narrow')), as said below
- second: float32 [1773312], P(('wide', 'narrow')), as said below
- rate: float32 [1], replicated, may hold values from 0.5 to 1
- step: int32 [1], replicated, may hold values from 2 to 20
Outputs:
- layer_out: bfloat16 [65536, 384], P(('wide', 'narrow'))
- grad_input: bfloat16 [65536, 384], P(('wide', 'narrow'))
- master_new: float32 [1773312], P(('wide', 'narrow'))
- first_new: float32 [1773312], P(('wide', 'narrow'))
- second_new: float32 [1773312], P(('wide', 'narrow'))
- copy_new: bfloat16 [1773312], P(('wide', 'narrow'))
Inputs may be any that keep to these rules, and one draw needn't show every extreme that they name: The visible patches of a sample are its first counts[s] slots; the others are padding. `first`: first moments of both signs. `second`: second moments, all positive.
All inputs are finite; a program needn't handle non-finite values.
Results may differ from a plain program's by a relative error of at most 0.007.
The roundings to bfloat16 on the way count: a program that leaves them out, or rounds other values in their place, can miss the bound.
Values may be sent and summed in bfloat16 or wider, within the bound.
No kernel may reach another device: no remote copies, remote signals or barrier semaphores. Data moves between devices by JAX's collectives and lax.ppermute only.
A program may use at most 192 MiB of HBM per device.

v0:
```python
import functools

import jax
import jax.numpy as jnp
from jax import lax
from jax.experimental import pallas as pl
from jax.experimental.pallas import tpu as pltpu
from jax.sharding import PartitionSpec as P

D = 384
FF = 1536
HEADS = 6
HEAD_DIM = 64
PATCHES = 64
LANES = 128
PAIRS = HEADS // 2
EPS = 1e-06
AXES = ("wide", "narrow")
QKV_ROWS = 3 * D * D // LANES
OUT_ROWS = D * D // LANES
UP_ROWS = D * FF // LANES
VEC_ROWS = (6 * D + FF) // LANES
FLAT_ROWS = QKV_ROWS + OUT_ROWS + 2 * UP_ROWS + VEC_ROWS
BASE_OUT = QKV_ROWS
BASE_UP = BASE_OUT + OUT_ROWS
BASE_DOWN = BASE_UP + UP_ROWS
BASE_VEC = BASE_DOWN + UP_ROWS
VECTORS = ("gain_one", "shift_one", "bias_out", "gain_two", "shift_two", "bias_up", "bias_down")
VMEM_LIMIT = 60 * 1024 * 1024


def round_up(value, step):
    return (value + step - 1) // step * step


def chunk_shape(shard):
    return round_up(shard + 1024, 16 * LANES) // LANES


def dot(left, right, left_dim, right_dim):
    return lax.dot_general(
        left, right, (((left_dim,), (right_dim,)), ((), ())), preferred_element_type=jnp.float32
    )


def vector_width(name):
    return FF if name == "bias_up" else D


def vector_row(name):
    return VECTORS.index(name)


def unpack_kernel(shard, devices, chunks, w_qkv, w_out, w_up, w_down, vectors, flat):
    rows = chunks.shape[1]
    for owner in range(devices):
        start = owner * shard // 1024 * 8
        piece = chunks[owner].astype(jnp.float32)
        if owner == 0:
            flat[pl.ds(start, rows), :] = piece
        else:
            flat[pl.ds(start, 8), :] = flat[pl.ds(start, 8), :] + piece[:8]
            flat[pl.ds(start + 8, rows - 8), :] = piece[8:]
    for ref, base in ((w_qkv, 0), (w_out, BASE_OUT), (w_up, BASE_UP), (w_down, BASE_DOWN)):
        height, width = ref.shape
        blocks = width // LANES
        for block in range(blocks):
            ref[:, block * LANES : (block + 1) * LANES] = flat[
                pl.ds(base + block, height, stride=blocks), :
            ].astype(jnp.bfloat16)
    row = BASE_VEC
    for index, name in enumerate(VECTORS):
        for block in range(vector_width(name) // LANES):
            vectors[index : index + 1, block * LANES : (block + 1) * LANES] = flat[
                row : row + 1, :
            ]
            row += 1


def unpack(chunks, shard, devices):
    rows = chunks.shape[1]
    flat_rows = max((devices - 1) * shard // 1024 * 8 + rows, round_up(FLAT_ROWS, 8))
    low = jnp.bfloat16
    return pl.pallas_call(
        functools.partial(unpack_kernel, shard, devices),
        name="unpack",
        out_shape=(
            jax.ShapeDtypeStruct((D, 3 * D), low),
            jax.ShapeDtypeStruct((D, D), low),
            jax.ShapeDtypeStruct((D, FF), low),
            jax.ShapeDtypeStruct((FF, D), low),
            jax.ShapeDtypeStruct((8, FF), jnp.float32),
        ),
        scratch_shapes=[pltpu.VMEM((flat_rows, LANES), jnp.float32)],
        compiler_params=pltpu.CompilerParams(vmem_limit_bytes=VMEM_LIMIT),
    )(chunks)


def vector(vectors, name):
    index = vector_row(name)
    return vectors[index : index + 1, : vector_width(name)]


def normalize(values):
    center = values - jnp.mean(values, axis=-1, keepdims=True)
    spread = jnp.mean(center * center, axis=-1, keepdims=True)
    scale = lax.rsqrt(spread + EPS)
    return center * scale, scale


def norm_back(grad, gain, hat, scale):
    inner = grad * gain
    mean_inner = jnp.mean(inner, axis=-1, keepdims=True)
    mean_cross = jnp.mean(inner * hat, axis=-1, keepdims=True)
    return scale * (inner - mean_inner - hat * mean_cross)


def column_sum(values):
    return jnp.sum(values, axis=0, keepdims=True)


def pair_lanes(rows):
    return lax.broadcasted_iota(jnp.int32, (rows, LANES), 1)


def block_diagonal(values, first_half):
    zero = jnp.zeros_like(values)
    return jnp.concatenate(
        [jnp.where(first_half, values, zero), jnp.where(first_half, zero, values)], axis=0
    )


def spread_halves(reduce, values, first_half, fill):
    first = reduce(jnp.where(first_half, values, fill), axis=-1, keepdims=True)
    second = reduce(jnp.where(first_half, fill, values), axis=-1, keepdims=True)
    return jnp.where(first_half, first, second)


def attention_kernel(
    counts, tokens, w_qkv, w_out, vectors, packed, chance, mixed, hidden
):
    block_rows = tokens.shape[0]
    samples = block_rows // PATCHES
    first_sample = pl.program_id(0) * samples
    inputs = tokens[...].astype(jnp.float32)
    hat, _ = normalize(inputs)
    normed = hat * vector(vectors, "gain_one") + vector(vectors, "shift_one")
    packed[...] = dot(normed.astype(jnp.bfloat16), w_qkv[...], 1, 0).astype(jnp.bfloat16)
    lanes = pair_lanes(PATCHES)
    first_half = lanes < HEAD_DIM
    keys_at = lanes % HEAD_DIM
    for sample in range(samples):
        rows = slice(sample * PATCHES, (sample + 1) * PATCHES)
        visible = keys_at < counts[first_sample + sample]
        for pair in range(PAIRS):
            at = pair * LANES
            queries = packed[rows, at : at + LANES]
            keys = block_diagonal(packed[rows, D + at : D + at + LANES], first_half)
            values = block_diagonal(packed[rows, 2 * D + at : 2 * D + at + LANES], first_half)
            scores = dot(queries, keys, 1, 1) * HEAD_DIM**-0.5
            scores = jnp.where(visible, scores, -1e30)
            largest = spread_halves(jnp.max, scores, first_half, -jnp.inf)
            exponent = jnp.exp(scores - largest)
            total = spread_halves(jnp.sum, exponent, first_half, 0.0)
            attend = exponent / total
            chance[rows, at : at + LANES] = attend
            mixed[rows, at : at + LANES] = dot(attend.astype(jnp.bfloat16), values, 1, 0).astype(
                jnp.bfloat16
            )
    hidden[...] = inputs + dot(mixed[...], w_out[...], 1, 0) + vector(vectors, "bias_out")


def attention(counts, tokens, w_qkv, w_out, vectors, block):
    rows = tokens.shape[0]

    def by_rows(width):
        return pl.BlockSpec((block, width), lambda i, counts: (i, 0))

    def whole(array):
        return pl.BlockSpec(array.shape, lambda i, counts: (0, 0))

    return pl.pallas_call(
        attention_kernel,
        name="attention",
        grid_spec=pltpu.PrefetchScalarGridSpec(
            num_scalar_prefetch=1,
            grid=(rows // block,),
            in_specs=[by_rows(D), whole(w_qkv), whole(w_out), whole(vectors)],
            out_specs=[by_rows(3 * D), by_rows(D), by_rows(D), by_rows(D)],
        ),
        out_shape=(
            jax.ShapeDtypeStruct((rows, 3 * D), jnp.bfloat16),
            jax.ShapeDtypeStruct((rows, D), jnp.float32),
            jax.ShapeDtypeStruct((rows, D), jnp.bfloat16),
            jax.ShapeDtypeStruct((rows, D), jnp.float32),
        ),
        compiler_params=pltpu.CompilerParams(vmem_limit_bytes=VMEM_LIMIT),
    )(counts, tokens, w_qkv, w_out, vectors)


def visible_rows(counts, first_sample, samples):
    slots = lax.broadcasted_iota(jnp.int32, (PATCHES, 1), 0)
    return jnp.concatenate(
        [
            jnp.where(slots < counts[first_sample + sample], 1.0, 0.0)
            for sample in range(samples)
        ],
        axis=0,
    )


def feed_kernel(
    step_columns,
    counts,
    hidden,
    cotangent,
    w_up,
    w_down,
    vectors,
    result,
    grad_hidden,
    grad_up,
    grad_down,
    grad_vectors,
    acc_up,
    acc_down,
):
    step = pl.program_id(0)
    block_rows = hidden.shape[0]
    samples = block_rows // PATCHES

    @pl.when(step == 0)
    def _():
        acc_up[...] = jnp.zeros_like(acc_up)
        acc_down[...] = jnp.zeros_like(acc_down)
        grad_vectors[...] = jnp.zeros_like(grad_vectors)

    def add_vector(name, values):
        index = vector_row(name)
        width = vector_width(name)
        grad_vectors[index : index + 1, :width] += column_sum(values)

    through = hidden[...]
    hat, scale = normalize(through)
    gain = vector(vectors, "gain_two")
    normed = (hat * gain + vector(vectors, "shift_two")).astype(jnp.bfloat16)
    grad_out = cotangent[...].astype(jnp.float32) * visible_rows(counts, step * samples, samples)
    grad_out_low = grad_out.astype(jnp.bfloat16)
    add_vector("bias_down", grad_out)
    total = through + vector(vectors, "bias_down")
    grad_normed = jnp.zeros_like(through)
    bias_up = vector(vectors, "bias_up")
    for at in range(0, FF, step_columns):
        columns = slice(at, at + step_columns)
        upward = dot(normed, w_up[:, columns], 1, 0) + bias_up[:, columns]
        below = 0.5 * (1.0 + lax.erf(upward * 0.5**0.5))
        active = (upward * below).astype(jnp.bfloat16)
        slope = below + upward * (jnp.exp(-0.5 * upward * upward) * (0.5 / jnp.pi) ** 0.5)
        total = total + dot(active, w_down[columns, :], 1, 0)
        grad_upward = dot(grad_out_low, w_down[columns, :], 1, 1) * slope
        grad_upward_low = grad_upward.astype(jnp.bfloat16)
        grad_vectors[5:6, columns] += column_sum(grad_upward_low.astype(jnp.float32))
        acc_down[columns, :] += dot(active, grad_out_low, 0, 0)
        acc_up[:, columns] += dot(normed, grad_upward_low, 0, 0)
        grad_normed = grad_normed + dot(grad_upward_low, w_up[:, columns], 1, 1)
    result[...] = total.astype(jnp.bfloat16)
    add_vector("gain_two", grad_normed * hat)
    add_vector("shift_two", grad_normed)
    grad_hidden[...] = grad_out + norm_back(grad_normed, gain, hat, scale)

    @pl.when(step == pl.num_programs(0) - 1)
    def _():
        flatten(acc_up, grad_up, 0)
        flatten(acc_down, grad_down, 0)


def flatten(matrix, flat, base):
    height, width = matrix.shape
    blocks = width // LANES
    for block in range(blocks):
        flat[pl.ds(base + block, height, stride=blocks), :] = matrix[
            :, block * LANES : (block + 1) * LANES
        ]


def feed(counts, hidden, cotangent, w_up, w_down, vectors, block, step_columns):
    rows = hidden.shape[0]

    def by_rows(width):
        return pl.BlockSpec((block, width), lambda i, counts: (i, 0))

    def whole(shape):
        return pl.BlockSpec(shape, lambda i, counts: (0, 0))

    return pl.pallas_call(
        functools.partial(feed_kernel, step_columns),
        name="feed",
        grid_spec=pltpu.PrefetchScalarGridSpec(
            num_scalar_prefetch=1,
            grid=(rows // block,),
            in_specs=[by_rows(D), by_rows(D), whole(w_up.shape), whole(w_down.shape), whole(vectors.shape)],
            out_specs=[by_rows(D), by_rows(D), whole((UP_ROWS, LANES)), whole((UP_ROWS, LANES)), whole((8, FF))],
            scratch_shapes=[pltpu.VMEM((D, FF), jnp.float32), pltpu.VMEM((FF, D), jnp.float32)],
        ),
        out_shape=(
            jax.ShapeDtypeStruct((rows, D), jnp.bfloat16),
            jax.ShapeDtypeStruct((rows, D), jnp.float32),
            jax.ShapeDtypeStruct((UP_ROWS, LANES), jnp.float32),
            jax.ShapeDtypeStruct((UP_ROWS, LANES), jnp.float32),
            jax.ShapeDtypeStruct((8, FF), jnp.float32),
        ),
        compiler_params=pltpu.CompilerParams(vmem_limit_bytes=VMEM_LIMIT),
    )(counts, hidden, cotangent, w_up, w_down, vectors)


def attention_back_kernel(
    tokens,
    packed,
    chance,
    mixed,
    grad_hidden,
    w_qkv,
    w_out,
    vectors,
    grad_input,
    grad_qkv,
    grad_w_out,
    grad_vectors,
    acc_qkv,
    acc_out,
    grad_packed,
):
    step = pl.program_id(0)
    samples = tokens.shape[0] // PATCHES

    @pl.when(step == 0)
    def _():
        acc_qkv[...] = jnp.zeros_like(acc_qkv)
        acc_out[...] = jnp.zeros_like(acc_out)
        grad_vectors[...] = jnp.zeros_like(grad_vectors)

    def add_vector(name, values):
        index = vector_row(name)
        grad_vectors[index : index + 1, :D] += column_sum(values)

    grad_through = grad_hidden[...]
    grad_low = grad_through.astype(jnp.bfloat16)
    add_vector("bias_out", grad_low.astype(jnp.float32))
    acc_out[...] += dot(mixed[...], grad_low, 0, 0)
    grad_mixed = dot(grad_low, w_out[...], 1, 1).astype(jnp.bfloat16)
    first_half = pair_lanes(PATCHES) < HEAD_DIM
    factor = HEAD_DIM**-0.5
    for sample in range(samples):
        rows = slice(sample * PATCHES, (sample + 1) * PATCHES)
        for pair in range(PAIRS):
            at = pair * LANES
            queries = packed[rows, at : at + LANES]
            keys = block_diagonal(packed[rows, D + at : D + at + LANES], first_half)
            values = block_diagonal(packed[rows, 2 * D + at : 2 * D + at + LANES], first_half)
            attend = chance[rows, at : at + LANES]
            grad_pair = grad_mixed[rows, at : at + LANES]
            grad_attend = dot(grad_pair, values, 1, 1)
            inner = spread_halves(jnp.sum, attend * grad_attend, first_half, 0.0)
            grad_scores = (attend * (grad_attend - inner)).astype(jnp.bfloat16)
            grad_queries = dot(grad_scores, keys, 1, 0) * factor
            grad_keys = dot(grad_scores, queries, 0, 0)
            grad_keys = jnp.where(first_half, grad_keys[:PATCHES], grad_keys[PATCHES:]) * factor
            grad_values = dot(attend.astype(jnp.bfloat16), grad_pair, 0, 0)
            grad_values = jnp.where(first_half, grad_values[:PATCHES], grad_values[PATCHES:])
            grad_packed[rows, at : at + LANES] = grad_queries.astype(jnp.bfloat16)
            grad_packed[rows, D + at : D + at + LANES] = grad_keys.astype(jnp.bfloat16)
            grad_packed[rows, 2 * D + at : 2 * D + at + LANES] = grad_values.astype(jnp.bfloat16)
    hat, scale = normalize(tokens[...].astype(jnp.float32))
    gain = vector(vectors, "gain_one")
    normed = (hat * gain + vector(vectors, "shift_one")).astype(jnp.bfloat16)
    acc_qkv[...] += dot(normed, grad_packed[...], 0, 0)
    grad_normed = dot(grad_packed[...], w_qkv[...], 1, 1)
    add_vector("gain_one", grad_normed * hat)
    add_vector("shift_one", grad_normed)
    grad_input[...] = (grad_through + norm_back(grad_normed, gain, hat, scale)).astype(
        jnp.bfloat16
    )

    @pl.when(step == pl.num_programs(0) - 1)
    def _():
        flatten(acc_qkv, grad_qkv, 0)
        flatten(acc_out, grad_w_out, 0)


def attention_back(tokens, packed, chance, mixed, grad_hidden, w_qkv, w_out, vectors, block):
    rows = tokens.shape[0]

    def by_rows(width):
        return pl.BlockSpec((block, width), lambda i: (i, 0))

    def whole(shape):
        return pl.BlockSpec(shape, lambda i: (0, 0))

    return pl.pallas_call(
        attention_back_kernel,
        name="attention_back",
        grid=(rows // block,),
        in_specs=[
            by_rows(D),
            by_rows(3 * D),
            by_rows(D),
            by_rows(D),
            by_rows(D),
            whole(w_qkv.shape),
            whole(w_out.shape),
            whole(vectors.shape),
        ],
        out_specs=[by_rows(D), whole((QKV_ROWS, LANES)), whole((OUT_ROWS, LANES)), whole((8, FF))],
        scratch_shapes=[
            pltpu.VMEM((D, 3 * D), jnp.float32),
            pltpu.VMEM((D, D), jnp.float32),
            pltpu.VMEM((block, 3 * D), jnp.bfloat16),
        ],
        out_shape=(
            jax.ShapeDtypeStruct((rows, D), jnp.bfloat16),
            jax.ShapeDtypeStruct((QKV_ROWS, LANES), jnp.float32),
            jax.ShapeDtypeStruct((OUT_ROWS, LANES), jnp.float32),
            jax.ShapeDtypeStruct((8, FF), jnp.float32),
        ),
        compiler_params=pltpu.CompilerParams(vmem_limit_bytes=VMEM_LIMIT),
    )(tokens, packed, chance, mixed, grad_hidden, w_qkv, w_out, vectors)


def pack_kernel(shard, devices, grad_qkv, grad_out, grad_up, grad_down, vectors, chunks, flat):
    rows = chunks.shape[1]
    flat[0:QKV_ROWS, :] = grad_qkv[...]
    flat[BASE_OUT : BASE_OUT + OUT_ROWS, :] = grad_out[...]
    flat[BASE_UP : BASE_UP + UP_ROWS, :] = grad_up[...]
    flat[BASE_DOWN : BASE_DOWN + UP_ROWS, :] = grad_down[...]
    row = BASE_VEC
    for index, name in enumerate(VECTORS):
        for block in range(vector_width(name) // LANES):
            flat[row : row + 1, :] = vectors[
                index : index + 1, block * LANES : (block + 1) * LANES
            ]
            row += 1
    flat[row:, :] = jnp.zeros_like(flat[row:, :])
    for owner in range(devices):
        start = owner * shard // 1024 * 8
        chunks[owner] = flat[start : start + rows, :].astype(jnp.bfloat16)


def pack(grad_qkv, grad_out, grad_up, grad_down, vectors, shard, devices):
    rows = chunk_shape(shard)
    flat_rows = max((devices - 1) * shard // 1024 * 8 + rows, round_up(FLAT_ROWS, 8))
    return pl.pallas_call(
        functools.partial(pack_kernel, shard, devices),
        name="pack",
        out_shape=jax.ShapeDtypeStruct((devices, rows, LANES), jnp.bfloat16),
        scratch_shapes=[pltpu.VMEM((flat_rows, LANES), jnp.float32)],
        compiler_params=pltpu.CompilerParams(vmem_limit_bytes=VMEM_LIMIT),
    )(grad_qkv, grad_out, grad_up, grad_down, vectors)


def step_scale(position):
    bound_one = QKV_ROWS * LANES
    bound_two = BASE_UP * LANES
    bound_three = BASE_DOWN * LANES
    bound_four = BASE_VEC * LANES
    scale = jnp.where(
        position < bound_one,
        D ** (-0.5),
        jnp.where(
            position < bound_two,
            (D // 8) ** (-0.5),
            jnp.where(
                position < bound_three,
                D ** (-0.5),
                jnp.where(position < bound_four, FF ** (-0.5), 0.1),
            ),
        ),
    )
    decay = jnp.where(position < bound_four, 0.05, 0.0)
    return (scale, decay)


def on_device(tokens, counts, cotangent, master, first, second, rate, step):
    shard = master.shape[0]
    devices = lax.axis_size(AXES)
    me = lax.axis_index(AXES)
    rows = chunk_shape(shard)
    offset = me * shard % 1024
    own = lax.dynamic_update_slice(
        jnp.zeros((rows * LANES,), jnp.bfloat16), master.astype(jnp.bfloat16), (offset,)
    ).reshape(rows, LANES)
    chunks = lax.all_gather(lax.all_gather(own, "narrow"), "wide").reshape(devices, rows, LANES)
    w_qkv, w_out, w_up, w_down, vectors = unpack(chunks, shard, devices)
    packed, chance, mixed, hidden = attention(counts, tokens, w_qkv, w_out, vectors, 512)
    result, grad_hidden, grad_up, grad_down, vectors_two = feed(
        counts, hidden, cotangent, w_up, w_down, vectors, 256, 512
    )
    grad_input, grad_qkv, grad_out, vectors_one = attention_back(
        tokens, packed, chance, mixed, grad_hidden, w_qkv, w_out, vectors, 512
    )
    sent = pack(
        grad_qkv, grad_out, grad_up, grad_down, vectors_one + vectors_two, shard, devices
    )
    sent = sent.reshape(lax.axis_size("wide"), lax.axis_size("narrow"), rows, LANES)
    reduced = lax.psum_scatter(
        lax.psum_scatter(sent, "wide", scatter_dimension=0), "narrow", scatter_dimension=0
    )
    reduced = lax.dynamic_slice(
        reduced.astype(jnp.float32).reshape(rows * LANES), (offset,), (shard,)
    )
    position = me * shard + jnp.arange(shard, dtype=jnp.int32)
    first_new = 0.5 * first + 0.5 * reduced
    second_new = 0.5 * second + 0.5 * reduced * reduced
    correct = 1.0 - jnp.power(jnp.float32(0.5), step[0].astype(jnp.float32))
    scale, decay = step_scale(position)
    moved = first_new / correct / (jnp.sqrt(second_new / correct) + 1e-08)
    master_new = master - rate[0] * scale * (moved + decay * master)
    return (
        result,
        grad_input,
        master_new,
        first_new,
        second_new,
        master_new.astype(jnp.bfloat16),
    )


def solution(mesh):
    split = P(AXES)
    by_rows = P(AXES, None)
    return jax.shard_map(
        on_device,
        mesh=mesh,
        in_specs=(by_rows, split, by_rows, split, split, split, P(), P()),
        out_specs=(by_rows, by_rows, split, split, split, split),
        check_vma=False,
    )
```

profile of v0, /device:TPU:0, one launch (start us, length us, event | category | flops | bytes accessed | tf_op | source)
XLA Modules:
  0.0 277.9 jit_solution(1047622873514937595)
XLA Ops:
  7.2 0.0 all-gather.3.cloned.1.call-start
  7.2 1.0 convert_element_type.17
  8.2 1.1 dynamic_update_slice.3
  9.4 6.9 %all_gather.9 = bf16[2,448,128]{2,1,0:T(8,128)(2,1)} all-gather(bf16[1,448,128]{2,1,0:T(8,128)(2,1)S(1)} %bitcast.9), channel_id=1, replica_groups=mesh['wide'=16,'narrow'=2] {'narrow'}, dimensions={0}, use_global_device_ids=true | all-gather | bytes 344064 | tf_op jit(solution)/shard_map/all_gather | solution.py:491
  16.2 0.0 all-gather.3.cloned.1.call-update
  16.3 0.0 reduce-scatter.3.cloned.1.call-start
  16.3 49.1 %all-gather.3.cloned.1.call-done.chunks = bf16[32,448,128]{2,1,0:T(8,128)(2,1)} async-done(((bf16[2,448,128]{2,1,0:T(8,128)(2,1)}), bf16[32,448,128]{2,1,0:T(8,128)(2,1)}) %all-gather.3.cloned.1.call-update) | async-done | bytes 3670032 | tf_op jit(solution)/shard_map/all_gather | solution.py:491
  65.4 4.4 %unpack.1 = (bf16[384,1152]{1,0:T(8,128)(2,1)}, bf16[384,384]{1,0:T(8,128)(2,1)}, bf16[384,1536]{1,0:T(8,128)(2,1)}, bf16[1536,384]{1,0:T(8,128)(2,1)}, f32[8,1536]{1,0:T(8,128)}) custom-call(bf16[32,448,128]{2,1,0:T(8,128)(2,1)} %all-gather.3.cloned.1.call-done.chunks), custom_call_target="tpu_custom_call" | custom-call | tf_op jit(solution)/shard_map/unpack/pallas_call | solution.py:84
  69.8 39.2 %attention.1 = (bf16[2048,1152]{1,0:T(8,128)(2,1)}, f32[2048,384]{1,0:T(8,128)}, bf16[2048,384]{1,0:T(8,128)(2,1)}, f32[2048,384]{1,0:T(8,128)}) custom-call(s32[32]{0:T(128)} %counts.3, bf16[2048,384]{1,0:T(8,128)(2,1)} %tokens.3, bf16[384,1152]{1,0:T(8,128)(2,1)} %get-tuple-element.24.w_qkv, bf16[384,384]{1,0:T(8,128)(2,1)} %get-tuple-element.25.w_out, ...), custom_call_target="tpu_custom_call" | custom-call | tf_op jit(solution)/shard_map/attention/pallas_call | solution.py:182
  109.0 31.3 %feed.1 = (bf16[2048,384]{1,0:T(8,128)(2,1)}, f32[2048,384]{1,0:T(8,128)}, f32[4608,128]{1,0:T(8,128)}, f32[4608,128]{1,0:T(8,128)}, f32[8,1536]{1,0:T(8,128)}) custom-call(s32[32]{0:T(128)} %counts.3, f32[2048,384]{1,0:T(8,128)} %get-tuple-element.27.hidden, bf16[2048,384]{1,0:T(8,128)(2,1)} %cotangent.1, bf16[384,1536]{1,0:T(8,128)(2,1)} %get-tuple-element.28.w_up, ...), custom_call_target="tpu_custom_call" | custom-call | tf_op jit(solution)/shard_map/feed/pallas_call | solution.py:295
  140.3 0.0 copy-start.3
  140.3 41.4 %attention_back.1 = (bf16[2048,384]{1,0:T(8,128)(2,1)}, f32[3456,128]{1,0:T(8,128)}, f32[1152,128]{1,0:T(8,128)}, f32[8,1536]{1,0:T(8,128)}) custom-call(bf16[2048,384]{1,0:T(8,128)(2,1)} %tokens.3, bf16[2048,1152]{1,0:T(8,128)(2,1)} %get-tuple-element.31.packed, f32[2048,384]{1,0:T(8,128)} %get-tuple-element.32.chance, ...), custom_call_target="tpu_custom_call" | custom-call | tf_op jit(solution)/shard_map/attention_back/pallas_call | solution.py:399
  181.7 0.0 copy-done.3
  181.7 1.4 add.44.vectors
  183.1 5.7 %pack.1 = bf16[32,448,128]{2,1,0:T(8,128)(2,1)} custom-call(f32[3456,128]{1,0:T(8,128)} %get-tuple-element.36.grad_qkv, f32[1152,128]{1,0:T(8,128)} %get-tuple-element.37.grad_out, f32[4608,128]{1,0:T(8,128)} %get-tuple-element.38.grad_up, f32[4608,128]{1,0:T(8,128)} %get-tuple-element.39.grad_down, f32[8,1536]{1,0:T(8,128)} %add.44.vectors), custom_call_target="tpu_custom_call" | custom-call | tf_op jit(solution)/shard_map/pack/pallas_call | solution.py:451
  188.9 0.0 copy-start
  188.9 0.0 copy-start.1
  188.9 0.0 copy-start.2
  188.9 0.0 reduce-scatter.3.cloned.1.call-update
  188.9 0.0 reduce-scatter.5.cloned.1.call-start
  188.9 67.8 %reduce-scatter.3.cloned.1.call-done = bf16[1,2,448,128]{3,2,1,0:T(8,128)(2,1)} async-done(((bf16[16,2,448,128]{3,2,1,0:T(8,128)(2,1)}), bf16[1,2,448,128]{3,2,1,0:T(8,128)(2,1)}) %reduce-scatter.3.cloned.1.call-update) | async-done | bytes 229392 | tf_op jit(solution)/shard_map/reduce_scatter | solution.py:505
  256.8 0.0 reduce-scatter.5.cloned.1.call-update
  258.1 11.2 %reduce-scatter.5.cloned.1.call-done = bf16[1,448,128]{2,1,0:T(8,128)(2,1)} async-done(((bf16[2,448,128]{2,1,0:T(8,128)(2,1)}), bf16[1,448,128]{2,1,0:T(8,128)(2,1)}) %reduce-scatter.5.cloned.1.call-update) | async-done | bytes 114704 | tf_op jit(solution)/shard_map/reduce_scatter | solution.py:504
  269.3 0.0 copy-done
  269.3 0.0 copy-done.1
  269.3 0.0 copy-done.2
  269.3 2.1 fusion.5
  (1 shorter events, 0.0 us)
Async XLA Ops:
  7.2 58.2 %all-gather.3.cloned.1.call-start = ((), (), s32[]{:S(2)}) async-start(), calls=%async_computation.4 | async-start | bytes 3899392 | tf_op jit(solution)/shard_map/all_gather | solution.py:491
  16.3 240.5 %reduce-scatter.3.cloned.1.call-start = ((), (), s32[]{:S(2)}) async-start(), calls=%async_computation.2 | async-start | bytes 3899392 | tf_op jit(solution)/shard_map/reduce_scatter | solution.py:505
  140.3 41.4 %copy-start.3 = (f32[8,1536]{1,0:T(8,128)S(1)}, f32[8,1536]{1,0:T(8,128)}, u32[]{:S(2)}) copy-start(f32[8,1536]{1,0:T(8,128)} %get-tuple-element.41) | copy-start | bytes 147460
  188.9 80.5 %copy-start = (f32[55416]{0:T(1024)S(1)}, f32[55416]{0:T(1024)}, u32[]{:S(2)}) copy-start(f32[55416]{0:T(1024)} %param.11) | copy-start | bytes 664996
  188.9 80.5 %copy-start.1 = (f32[55416]{0:T(1024)S(1)}, f32[55416]{0:T(1024)}, u32[]{:S(2)}) copy-start(f32[55416]{0:T(1024)} %param.13) | copy-start | bytes 664996
  188.9 80.5 %copy-start.2 = (f32[55416]{0:T(1024)S(1)}, f32[55416]{0:T(1024)}, u32[]{:S(2)}) copy-start(f32[55416]{0:T(1024)} %param.12) | copy-start | bytes 664996
  188.9 80.4 %reduce-scatter.5.cloned.1.call-start = ((), (), s32[]{:S(2)}) async-start(), calls=%async_computation.3 | async-start | bytes 344064 | tf_op jit(solution)/shard_map/reduce_scatter | solution.py:504
Sparse Core Ops, SparseCore 0:
  16.4 48.9 all-gather.2
  189.0 67.6 reduce-scatter.2
  259.1 10.1 reduce-scatter.4
where the time goes:
time: 278 us
  waiting for transfers between devices  128 us (46%)
  Pallas kernels  122 us (44%)
  between operations  15.2 us (5%)
  blocking collectives  6.87 us (2%)
  other arithmetic  4.45 us (2%)
    reduce_scatter x1, waiting for transfers between devices, on_device(): lax.psum_scatter(sent, 'wide', scatter_dimension=0)  67.8 us
    all_gather x1, waiting for transfers between devices, on_device(): lax.all_gather(lax.all_gather(own, 'narrow'), 'wide')  49.1 us
    pallas_call x1, Pallas kernels, attention_back(): pl.pallas_call(attention_back_kernel, name='attention_back', grid=(rows /...  41.4 us
    pallas_call x1, Pallas kernels, attention(): pl.pallas_call(attention_kernel, name='attention', grid_spec=pltpu.Prefet...  39.2 us
    pallas_call x1, Pallas kernels, feed(): pl.pallas_call(functools.partial(feed_kernel, step_columns), name='feed',...  31.3 us
    reduce_scatter x1, waiting for transfers between devices, on_device(): lax.psum_scatter(lax.psum_scatter(sent, 'wide', scatter_dimension=0), 'na...  11.2 us
    all_gather x1, blocking collectives, on_device(): lax.all_gather(own, 'narrow')  6.87 us
    pallas_call x1, Pallas kernels, pack(): pl.pallas_call(functools.partial(pack_kernel, shard, devices), name='pack...  5.72 us
  transfers between devices with their start and end apart: 3, of which 3 were waited for; matrix products, arithmetic and copies ran while one was open for 0% of the time, Pallas kernels for 0%

commit v1 on v0

--- a/solution.py
+++ b/solution.py
@@ -1,4 +1,5 @@
 import functools
+import itertools
 
 import jax
 import jax.numpy as jnp
@@ -6,6 +7,7 @@
 from jax.experimental import pallas as pl
 from jax.experimental.pallas import tpu as pltpu
 from jax.sharding import PartitionSpec as P
+import numpy as np
 
 D = 384
 FF = 1536
@@ -33,7 +35,7 @@
     return (value + step - 1) // step * step
 
 
-def chunk_shape(shard):
+def chunk_rows(shard):
     return round_up(shard + 1024, 16 * LANES) // LANES
 
 
@@ -51,16 +53,75 @@
     return VECTORS.index(name)
 
 
-def unpack_kernel(shard, devices, chunks, w_qkv, w_out, w_up, w_down, vectors, flat):
-    rows = chunks.shape[1]
+def exchange_plan(wide, narrow):
+    devices = wide * narrow
+    core = narrow
+    bits = [1 << k for k in reversed(range(devices.bit_length() - 1)) if 1 << k != core]
+    half = (len(bits) + 1) // 2
+    rounds = []
+    for first, second in itertools.zip_longest(bits[:half], bits[half:]):
+        if second is None:
+            rounds.append((first, first))
+        else:
+            rounds += [(first, second), (second, first)]
+    owners = np.zeros((devices, devices), np.int32)
+    for device in range(devices):
+        for owner in range(devices):
+            across = device ^ owner
+            holder = device ^ core if across & core else device
+            side = 1 if holder & core else 0
+            slot = devices // 2 if across & core else 0
+            for index, pair in enumerate(rounds):
+                if across & pair[side]:
+                    slot += 1 << index
+            owners[device, slot] = owner
+    swaps = [
+        [(device, device ^ pair[1 if device & core else 0]) for device in range(devices)]
+        for pair in rounds
+    ]
+    return swaps, [(device, device ^ core) for device in range(devices)], owners
+
+
+def gather_chunks(own, swaps, core_swap):
+    held = own[None]
+    for swap in swaps[:-1]:
+        held = jnp.concatenate([held, lax.ppermute(held, AXES, swap)], axis=0)
+    held_core = lax.ppermute(held, AXES, core_swap)
+    taken = lax.ppermute(held, AXES, swaps[-1])
+    taken_core = lax.ppermute(taken, AXES, core_swap)
+    return held, taken, held_core, taken_core
+
+
+def scatter_chunks(kept, sent, swaps, core_swap):
+    parts = [kept, lax.ppermute(sent, AXES, core_swap)]
+    for swap in reversed(swaps):
+        half = parts[0].shape[0] // 2
+        upper = sum(part[half:].astype(jnp.float32) for part in parts)
+        parts = [part[:half] for part in parts]
+        parts.append(lax.ppermute(upper.astype(jnp.bfloat16), AXES, swap))
+    return sum(part[0].astype(jnp.float32) for part in parts)
+
+
+def chunk_start(owner, shard):
+    return owner * shard // 1024 * 8
+
+
+def unpack_kernel(shard, starts, *refs):
+    pieces, (w_qkv, w_out, w_up, w_down, vectors, flat) = refs[:4], refs[4:]
+    rows = pieces[0].shape[1]
+    devices = 4 * pieces[0].shape[0]
+    sure = shard // 1024 * 8
     for owner in range(devices):
-        start = owner * shard // 1024 * 8
-        piece = chunks[owner].astype(jnp.float32)
-        if owner == 0:
-            flat[pl.ds(start, rows), :] = piece
-        else:
-            flat[pl.ds(start, 8), :] = flat[pl.ds(start, 8), :] + piece[:8]
-            flat[pl.ds(start + 8, rows - 8), :] = piece[8:]
+        start = chunk_start(owner, shard)
+        flat[start : start + 8, :] = jnp.zeros((8, LANES), jnp.float32)
+        flat[start + sure : start + rows, :] = jnp.zeros((rows - sure, LANES), jnp.float32)
+    for slot in range(devices):
+        source = pieces[slot * 4 // devices]
+        piece = source[slot % source.shape[0]].astype(jnp.float32)
+        start = pl.multiple_of(starts[slot], 8)
+        flat[pl.ds(start, 8), :] += piece[:8]
+        flat[pl.ds(start + 8, sure - 8), :] = piece[8:sure]
+        flat[pl.ds(start + sure, rows - sure), :] += piece[sure:]
     for ref, base in ((w_qkv, 0), (w_out, BASE_OUT), (w_up, BASE_UP), (w_down, BASE_DOWN)):
         height, width = ref.shape
         blocks = width // LANES
@@ -77,23 +138,30 @@
             row += 1
 
 
-def unpack(chunks, shard, devices):
-    rows = chunks.shape[1]
-    flat_rows = max((devices - 1) * shard // 1024 * 8 + rows, round_up(FLAT_ROWS, 8))
+def unpack(starts, pieces, shard):
+    quarter, rows, _ = pieces[0].shape
+    devices = 4 * quarter
+    flat_rows = max(chunk_start(devices - 1, shard) + rows, round_up(FLAT_ROWS, 8))
     low = jnp.bfloat16
+
+    def whole(shape):
+        return pl.BlockSpec(shape, lambda i, starts: (0,) * len(shape))
+
+    shapes = ((D, 3 * D), (D, D), (D, FF), (FF, D), (8, FF))
     return pl.pallas_call(
-        functools.partial(unpack_kernel, shard, devices),
+        functools.partial(unpack_kernel, shard),
         name="unpack",
-        out_shape=(
-            jax.ShapeDtypeStruct((D, 3 * D), low),
-            jax.ShapeDtypeStruct((D, D), low),
-            jax.ShapeDtypeStruct((D, FF), low),
-            jax.ShapeDtypeStruct((FF, D), low),
-            jax.ShapeDtypeStruct((8, FF), jnp.float32),
-        ),
-        scratch_shapes=[pltpu.VMEM((flat_rows, LANES), jnp.float32)],
+        grid_spec=pltpu.PrefetchScalarGridSpec(
+            num_scalar_prefetch=1,
+            grid=(1,),
+            in_specs=[whole(piece.shape) for piece in pieces],
+            out_specs=[whole(shape) for shape in shapes],
+            scratch_shapes=[pltpu.VMEM((flat_rows, LANES), jnp.float32)],
+        ),
+        out_shape=[jax.ShapeDtypeStruct(shape, low) for shape in shapes[:4]]
+        + [jax.ShapeDtypeStruct(shapes[4], jnp.float32)],
         compiler_params=pltpu.CompilerParams(vmem_limit_bytes=VMEM_LIMIT),
-    )(chunks)
+    )(starts, *pieces)
 
 
 def vector(vectors, name):
@@ -426,8 +494,10 @@
     )(tokens, packed, chance, mixed, grad_hidden, w_qkv, w_out, vectors)
 
 
-def pack_kernel(shard, devices, grad_qkv, grad_out, grad_up, grad_down, vectors, chunks, flat):
-    rows = chunks.shape[1]
+def pack_kernel(
+    starts, grad_qkv, grad_out, grad_up, grad_down, vectors, kept, sent, flat
+):
+    half, rows, _ = kept.shape
     flat[0:QKV_ROWS, :] = grad_qkv[...]
     flat[BASE_OUT : BASE_OUT + OUT_ROWS, :] = grad_out[...]
     flat[BASE_UP : BASE_UP + UP_ROWS, :] = grad_up[...]
@@ -440,21 +510,38 @@
             ]
             row += 1
     flat[row:, :] = jnp.zeros_like(flat[row:, :])
-    for owner in range(devices):
-        start = owner * shard // 1024 * 8
-        chunks[owner] = flat[start : start + rows, :].astype(jnp.bfloat16)
-
-
-def pack(grad_qkv, grad_out, grad_up, grad_down, vectors, shard, devices):
-    rows = chunk_shape(shard)
-    flat_rows = max((devices - 1) * shard // 1024 * 8 + rows, round_up(FLAT_ROWS, 8))
+    for slot in range(half):
+        kept[slot] = flat[pl.ds(pl.multiple_of(starts[slot], 8), rows), :]
+        sent[slot] = flat[pl.ds(pl.multiple_of(starts[half + slot], 8), rows), :].astype(
+            jnp.bfloat16
+        )
+
+
+def pack(starts, grad_qkv, grad_out, grad_up, grad_down, vectors, shard, devices):
+    rows = chunk_rows(shard)
+    flat_rows = max(chunk_start(devices - 1, shard) + rows, round_up(FLAT_ROWS, 8))
+    inputs = (grad_qkv, grad_out, grad_up, grad_down, vectors)
+
+    def whole(shape):
+        return pl.BlockSpec(shape, lambda i, starts: (0,) * len(shape))
+
+    shape = (devices // 2, rows, LANES)
     return pl.pallas_call(
-        functools.partial(pack_kernel, shard, devices),
+        pack_kernel,
         name="pack",
-        out_shape=jax.ShapeDtypeStruct((devices, rows, LANES), jnp.bfloat16),
-        scratch_shapes=[pltpu.VMEM((flat_rows, LANES), jnp.float32)],
+        grid_spec=pltpu.PrefetchScalarGridSpec(
+            num_scalar_prefetch=1,
+            grid=(1,),
+            in_specs=[whole(array.shape) for array in inputs],
+            out_specs=[whole(shape), whole(shape)],
+            scratch_shapes=[pltpu.VMEM((flat_rows, LANES), jnp.float32)],
+        ),
+        out_shape=(
+            jax.ShapeDtypeStruct(shape, jnp.float32),
+            jax.ShapeDtypeStruct(shape, jnp.bfloat16),
+        ),
         compiler_params=pltpu.CompilerParams(vmem_limit_bytes=VMEM_LIMIT),
-    )(grad_qkv, grad_out, grad_up, grad_down, vectors)
+    )(starts, *inputs)
 
 
 def step_scale(position):
@@ -483,13 +570,15 @@
     shard = master.shape[0]
     devices = lax.axis_size(AXES)
     me = lax.axis_index(AXES)
-    rows = chunk_shape(shard)
+    rows = chunk_rows(shard)
     offset = me * shard % 1024
     own = lax.dynamic_update_slice(
         jnp.zeros((rows * LANES,), jnp.bfloat16), master.astype(jnp.bfloat16), (offset,)
     ).reshape(rows, LANES)
-    chunks = lax.all_gather(lax.all_gather(own, "narrow"), "wide").reshape(devices, rows, LANES)
-    w_qkv, w_out, w_up, w_down, vectors = unpack(chunks, shard, devices)
+    swaps, core_swap, owners = exchange_plan(lax.axis_size("wide"), lax.axis_size("narrow"))
+    starts = jnp.asarray(chunk_start(owners, shard).astype(np.int32))[me]
+    pieces = gather_chunks(own, swaps, core_swap)
+    w_qkv, w_out, w_up, w_down, vectors = unpack(starts, pieces, shard)
     packed, chance, mixed, hidden = attention(counts, tokens, w_qkv, w_out, vectors, 512)
     result, grad_hidden, grad_up, grad_down, vectors_two = feed(
         counts, hidden, cotangent, w_up, w_down, vectors, 256, 512
@@ -497,15 +586,12 @@
     grad_input, grad_qkv, grad_out, vectors_one = attention_back(
         tokens, packed, chance, mixed, grad_hidden, w_qkv, w_out, vectors, 512
     )
-    sent = pack(
-        grad_qkv, grad_out, grad_up, grad_down, vectors_one + vectors_two, shard, devices
-    )
-    sent = sent.reshape(lax.axis_size("wide"), lax.axis_size("narrow"), rows, LANES)
-    reduced = lax.psum_scatter(
-        lax.psum_scatter(sent, "wide", scatter_dimension=0), "narrow", scatter_dimension=0
-    )
+    kept, sent = pack(
+        starts, grad_qkv, grad_out, grad_up, grad_down, vectors_one + vectors_two, shard, devices
+    )
+    reduced = scatter_chunks(kept, sent, swaps, core_swap)
     reduced = lax.dynamic_slice(
-        reduced.astype(jnp.float32).reshape(rows * LANES), (offset,), (shard,)
+        reduced.reshape(rows * LANES), (offset,), (shard,)
     )
     position = me * shard + jnp.arange(shard, dtype=jnp.int32)
     first_new = 0.5 * first + 0.5 * reduced

time: 278 us -> 210 us (0.76)
  waiting for transfers between devices: 128 us -> 56.5 us
  starting transfers between devices: 0.12 us -> 18.7 us
  between operations: 15.2 us -> 2.14 us
  blocking collectives: 6.87 us -> 0 us
    reduce_scatter x2 -> x0, waiting for transfers between devices: 79 us -> none  [the longest x1 67.8 us: on_device(): lax.psum_scatter(sent, 'wide', scatter_dimension=0)]
    ppermute x0 -> x11, waiting for transfers between devices: none -> 56.5 us  [the longest x4 25.8 us: scatter_chunks(): parts.append(lax.ppermute(upper.astype(jnp.bfloat16), AXES, swap))]
    all_gather x1 -> x0, waiting for transfers between devices: 49.1 us -> none  [on_device(): lax.all_gather(lax.all_gather(own, 'narrow'), 'wide')]
    ppermute x0 -> x11, starting transfers between devices: none -> 18.7 us  [the longest x3 8.48 us: gather_chunks(): held = jnp.concatenate([held, lax.ppermute(held, AXES, swap)], axis=0)]
    all_gather x1 -> x0, blocking collectives: 6.87 us -> none  [on_device(): lax.all_gather(own, 'narrow')]
  transfers between devices with their start and end apart: 3 -> 11, of which waited for: 3 -> 10; matrix products, arithmetic and copies ran while one was open for 0% -> 1% of each run, Pallas kernels for 0% -> 0%
where the time goes in v1:
time: 210 us
  Pallas kernels  124 us (59%)
  waiting for transfers between devices  56.5 us (27%)
  starting transfers between devices  18.7 us (9%)
  other arithmetic  6.03 us (3%)
  local copies, waits for them, and re-layouts  2.43 us (1%)
  between operations  2.14 us (1%)
    pallas_call x1, Pallas kernels, attention_back(): pl.pallas_call(attention_back_kernel, name='attention_back', grid=(rows /...  41.6 us
    pallas_call x1, Pallas kernels, attention(): pl.pallas_call(attention_kernel, name='attention', grid_spec=pltpu.Prefet...  39.2 us
    pallas_call x1, Pallas kernels, feed(): pl.pallas_call(functools.partial(feed_kernel, step_columns), name='feed',...  31.2 us
    ppermute x4, waiting for transfers between devices, scatter_chunks(): parts.append(lax.ppermute(upper.astype(jnp.bfloat16), AXES, swap))  25.8 us
    ppermute x3, waiting for transfers between devices, gather_chunks(): held = jnp.concatenate([held, lax.ppermute(held, AXES, swap)], axis=0)  14.1 us
    ppermute x1, waiting for transfers between devices, gather_chunks(): taken = lax.ppermute(held, AXES, swaps[-1])  11.4 us
    ppermute x3, starting transfers between devices, gather_chunks(): held = jnp.concatenate([held, lax.ppermute(held, AXES, swap)], axis=0)  8.48 us
    ppermute x4, starting transfers between devices, scatter_chunks(): parts.append(lax.ppermute(upper.astype(jnp.bfloat16), AXES, swap))  7.94 us
  transfers between devices with their start and end apart: 11, of which 10 were waited for; matrix products, arithmetic and copies ran while one was open for 1% of the time, Pallas kernels for 0%

profile of v1, /device:TPU:0, one launch (start us, length us, event | category | flops | bytes accessed | tf_op | source)
XLA Modules:
  0.0 209.9 jit_solution(13023234026499282841)
XLA Ops:
  0.6 1.0 convert_element_type.81
  1.6 1.1 dynamic_update_slice.3
  2.8 4.1 %collective-permute-start = (bf16[1,448,128]{2,1,0:T(8,128)(2,1)S(1)}, bf16[1,448,128]{2,1,0:T(8,128)(2,1)S(1)}, u32[]{:S(2)}, u32[]{:S(2)}) collective-permute-start(bf16[1,448,128]{2,1,0:T(8,128)(2,1)S(1)} %bitcast.8), channel_id=1, source_target_pairs={{0,16},{1,17},{2,6},{3,7},{4,20},{5,21},{6,2},{7,3},{8,24},{9,25},... | collective-permute-start | bytes 344072 | tf_op jit(solution)/shard_map/ppermute | solution.py:88
  6.9 2.8 %collective-permute-done = bf16[1,448,128]{2,1,0:T(8,128)(2,1)S(1)} collective-permute-done((bf16[1,448,128]{2,1,0:T(8,128)(2,1)S(1)}, bf16[1,448,128]{2,1,0:T(8,128)(2,1)S(1)}, u32[]{:S(2)}, u32[]{:S(2)}) %collective-permute-start) | collective-permute-done | bytes 114720 | tf_op jit(solution)/shard_map/ppermute | solution.py:88
  9.7 3.1 %collective-permute-start.1 = (bf16[2,448,128]{2,1,0:T(8,128)(2,1)S(1)}, bf16[2,448,128]{2,1,0:T(8,128)(2,1)S(1)}, u32[]{:S(2)}, u32[]{:S(2)}) collective-permute-start(bf16[2,448,128]{2,1,0:T(8,128)(2,1)S(1)} %pad_maximum_fusion.2), channel_id=1, source_target_pairs={{0,4},{1,5},{2,18},{3,19},{4,0},{5,1},{6,22},{7,23},{8,12},{9,13},... | collective-permute-start | bytes 688136 | tf_op jit(solution)/shard_map/ppermute | solution.py:88
  12.8 4.0 %collective-permute-done.1 = bf16[2,448,128]{2,1,0:T(8,128)(2,1)S(1)} collective-permute-done((bf16[2,448,128]{2,1,0:T(8,128)(2,1)S(1)}, bf16[2,448,128]{2,1,0:T(8,128)(2,1)S(1)}, u32[]{:S(2)}, u32[]{:S(2)}) %collective-permute-start.1) | collective-permute-done | bytes 229408 | tf_op jit(solution)/shard_map/ppermute | solution.py:88
  16.9 1.3 collective-permute-start.2
  18.1 7.3 %collective-permute-done.2 = bf16[4,448,128]{2,1,0:T(8,128)(2,1)S(1)} collective-permute-done((bf16[4,448,128]{2,1,0:T(8,128)(2,1)S(1)}, bf16[4,448,128]{2,1,0:T(8,128)(2,1)S(1)}, u32[]{:S(2)}, u32[]{:S(2)}) %collective-permute-start.2) | collective-permute-done | bytes 458784 | tf_op jit(solution)/shard_map/ppermute | solution.py:88
  25.4 0.1 pad_maximum_fusion.refs_0_
  25.5 0.0 copy-start.1
  25.5 2.1 %collective-permute-start.3 = (bf16[8,448,128]{2,1,0:T(8,128)(2,1)S(1)}, bf16[8,448,128]{2,1,0:T(8,128)(2,1)S(1)}, u32[]{:S(2)}, u32[]{:S(2)}) collective-permute-start(bf16[8,448,128]{2,1,0:T(8,128)(2,1)S(1)} %pad_maximum_fusion.refs_0_), channel_id=1, source_target_pairs={{0,1},{1,0},{2,10},{3,11},{4,5},{5,4},{6,14},{7,15},{8,9},{9,8},{1... | collective-permute-start | bytes 2752520 | tf_op jit(solution)/shard_map/ppermute | solution.py:90
  27.6 0.0 collective-permute-start.4
  27.6 11.4 %collective-permute-done.3.refs_1_ = bf16[8,448,128]{2,1,0:T(8,128)(2,1)S(1)} collective-permute-done((bf16[8,448,128]{2,1,0:T(8,128)(2,1)S(1)}, bf16[8,448,128]{2,1,0:T(8,128)(2,1)S(1)}, u32[]{:S(2)}, u32[]{:S(2)}) %collective-permute-start.3) | collective-permute-done | bytes 917536 | tf_op jit(solution)/shard_map/ppermute | solution.py:90
  39.0 0.0 copy-start.2
  39.0 0.0 collective-permute-start.5
  39.0 1.2 dynamic-slice_bitcast_fusion.starts
  40.2 0.0 collective-permute-done.4.refs_2_
  40.2 0.0 copy-start.3
  40.2 1.4 collective-permute-done.5.refs_3_
  41.6 0.0 copy-done.1
  41.6 0.0 copy-done.2
  41.6 0.0 copy-done.3
  41.6 5.1 %unpack.1 = (bf16[384,1152]{1,0:T(8,128)(2,1)}, bf16[384,384]{1,0:T(8,128)(2,1)}, bf16[384,1536]{1,0:T(8,128)(2,1)}, bf16[1536,384]{1,0:T(8,128)(2,1)}, f32[8,1536]{1,0:T(8,128)}) custom-call(s32[32]{0:T(128)} %dynamic-slice_bitcast_fusion.starts, bf16[8,448,128]{2,1,0:T(8,128)(2,1)} %copy-done.1, bf16[8,448,128]{2,1,0:T(8,128)(2,1)} %copy-done.2, ...), custom_call_target="tpu_custom_call" | custom-call | tf_op jit(solution)/shard_map/unpack/pallas_call | solution.py:151
  46.7 39.2 %attention.1 = (bf16[2048,1152]{1,0:T(8,128)(2,1)}, f32[2048,384]{1,0:T(8,128)}, bf16[2048,384]{1,0:T(8,128)(2,1)}, f32[2048,384]{1,0:T(8,128)}) custom-call(s32[32]{0:T(128)} %counts.3, bf16[2048,384]{1,0:T(8,128)(2,1)} %tokens.3, bf16[384,1152]{1,0:T(8,128)(2,1)} %get-tuple-element.26.w_qkv, bf16[384,384]{1,0:T(8,128)(2,1)} %get-tuple-element.27.w_out, ...), custom_call_target="tpu_custom_call" | custom-call | tf_op jit(solution)/shard_map/attention/pallas_call | solution.py:250
  85.9 31.2 %feed.1 = (bf16[2048,384]{1,0:T(8,128)(2,1)}, f32[2048,384]{1,0:T(8,128)}, f32[4608,128]{1,0:T(8,128)}, f32[4608,128]{1,0:T(8,128)}, f32[8,1536]{1,0:T(8,128)}) custom-call(s32[32]{0:T(128)} %counts.3, f32[2048,384]{1,0:T(8,128)} %get-tuple-element.29.hidden, bf16[2048,384]{1,0:T(8,128)(2,1)} %cotangent.1, bf16[384,1536]{1,0:T(8,128)(2,1)} %get-tuple-element.30.w_up, ...), custom_call_target="tpu_custom_call" | custom-call | tf_op jit(solution)/shard_map/feed/pallas_call | solution.py:363
  117.2 0.0 copy-start.7
  117.2 41.6 %attention_back.1 = (bf16[2048,384]{1,0:T(8,128)(2,1)}, f32[3456,128]{1,0:T(8,128)}, f32[1152,128]{1,0:T(8,128)}, f32[8,1536]{1,0:T(8,128)}) custom-call(bf16[2048,384]{1,0:T(8,128)(2,1)} %tokens.3, bf16[2048,1152]{1,0:T(8,128)(2,1)} %get-tuple-element.33.packed, f32[2048,384]{1,0:T(8,128)} %get-tuple-element.34.chance, ...), custom_call_target="tpu_custom_call" | custom-call | tf_op jit(solution)/shard_map/attention_back/pallas_call | solution.py:467
  158.8 0.0 copy-done.7
  158.8 1.4 add.99.vectors
  160.2 7.0 %pack.1 = (f32[16,448,128]{2,1,0:T(8,128)}, bf16[16,448,128]{2,1,0:T(8,128)(2,1)}) custom-call(s32[32]{0:T(128)} %dynamic-slice_bitcast_fusion.starts, f32[3456,128]{1,0:T(8,128)} %get-tuple-element.38.grad_qkv, f32[1152,128]{1,0:T(8,128)} %get-tuple-element.39.grad_out, f32[4608,128]{1,0:T(8,128)} %get-tuple-element.40.grad_up, ...), custom_call_target="tpu_custom_call" | custom-call | tf_op jit(solution)/shard_map/pack/pallas_call | solution.py:529
  167.3 0.1 collective-permute-start.6
  167.4 3.9 %collective-permute-done.6 = bf16[16,448,128]{2,1,0:T(8,128)(2,1)S(1)} collective-permute-done((bf16[16,448,128]{2,1,0:T(8,128)(2,1)}, bf16[16,448,128]{2,1,0:T(8,128)(2,1)S(1)}, u32[]{:S(2)}, u32[]{:S(2)}) %collective-permute-start.6) | collective-permute-done | bytes 1835040 | tf_op jit(solution)/shard_map/ppermute | solution.py:96
  171.3 0.0 copy-start
  171.3 1.9 add_convert_fusion
  173.1 2.1 collective-permute-start.7
  175.2 11.4 %collective-permute-done.7 = bf16[8,448,128]{2,1,0:T(8,128)(2,1)S(1)} collective-permute-done((bf16[8,448,128]{2,1,0:T(8,128)(2,1)S(1)}, bf16[8,448,128]{2,1,0:T(8,128)(2,1)S(1)}, u32[]{:S(2)}, u32[]{:S(2)}) %collective-permute-start.7) | collective-permute-done | bytes 917536 | tf_op jit(solution)/shard_map/ppermute | solution.py:101
  186.6 0.0 copy-done
  186.6 0.2 add_convert_fusion.1
  186.8 0.0 copy-start.4
  186.8 0.0 copy-start.5
  186.8 0.0 copy-start.6
  186.8 1.2 collective-permute-start.8
  188.0 7.3 %collective-permute-done.8 = bf16[4,448,128]{2,1,0:T(8,128)(2,1)S(1)} collective-permute-done((bf16[4,448,128]{2,1,0:T(8,128)(2,1)S(1)}, bf16[4,448,128]{2,1,0:T(8,128)(2,1)S(1)}, u32[]{:S(2)}, u32[]{:S(2)}) %collective-permute-start.8) | collective-permute-done | bytes 458784 | tf_op jit(solution)/shard_map/ppermute | solution.py:101
  195.4 0.1 add_convert_fusion.2
  195.5 2.0 collective-permute-start.9
  197.5 4.0 %collective-permute-done.9 = bf16[2,448,128]{2,1,0:T(8,128)(2,1)S(1)} collective-permute-done((bf16[2,448,128]{2,1,0:T(8,128)(2,1)S(1)}, bf16[2,448,128]{2,1,0:T(8,128)(2,1)S(1)}, u32[]{:S(2)}, u32[]{:S(2)}) %collective-permute-start.9) | collective-permute-done | bytes 229408 | tf_op jit(solution)/shard_map/ppermute | solution.py:101
  201.6 0.1 add_convert_fusion.3
  201.6 2.6 %collective-permute-start.10 = (bf16[1,448,128]{2,1,0:T(8,128)(2,1)S(1)}, bf16[1,448,128]{2,1,0:T(8,128)(2,1)S(1)}, u32[]{:S(2)}, u32[]{:S(2)}) collective-permute-start(bf16[1,448,128]{2,1,0:T(8,128)(2,1)S(1)} %add_convert_fusion.3), channel_id=1, source_target_pairs={{0,16},{1,17},{2,6},{3,7},{4,20},{5,21},{6,2},{7,3},{8,24},{9,25},... | collective-permute-start | bytes 344072 | tf_op jit(solution)/shard_map/ppermute | solution.py:101
  205.6 3.0 %collective-permute-done.10 = bf16[1,448,128]{2,1,0:T(8,128)(2,1)S(1)} collective-permute-done((bf16[1,448,128]{2,1,0:T(8,128)(2,1)S(1)}, bf16[1,448,128]{2,1,0:T(8,128)(2,1)S(1)}, u32[]{:S(2)}, u32[]{:S(2)}) %collective-permute-start.10) | collective-permute-done | bytes 114720 | tf_op jit(solution)/shard_map/ppermute | solution.py:101
  208.6 0.1 add_bitcast_fusion
  208.7 0.0 copy-done.4
  208.7 0.0 copy-done.5
  208.7 0.0 copy-done.6
  208.7 1.2 fusion.5
  (3 shorter events, 0.1 us)
Async XLA Ops:
  2.8 6.9 %collective-permute-start = (bf16[1,448,128]{2,1,0:T(8,128)(2,1)S(1)}, bf16[1,448,128]{2,1,0:T(8,128)(2,1)S(1)}, u32[]{:S(2)}, u32[]{:S(2)}) collective-permute-start(bf16[1,448,128]{2,1,0:T(8,128)(2,1)S(1)} %bitcast.8), channel_id=1, source_target_pairs={{0,16},{1,17},{2,6},{3,7},{4,20},{5,21},{6,2},{7,3},{8,24},{9,25},... | collective-permute-start | bytes 344072 | tf_op jit(solution)/shard_map/ppermute | solution.py:88
  9.7 7.1 %collective-permute-start.1 = (bf16[2,448,128]{2,1,0:T(8,128)(2,1)S(1)}, bf16[2,448,128]{2,1,0:T(8,128)(2,1)S(1)}, u32[]{:S(2)}, u32[]{:S(2)}) collective-permute-start(bf16[2,448,128]{2,1,0:T(8,128)(2,1)S(1)} %pad_maximum_fusion.2), channel_id=1, source_target_pairs={{0,4},{1,5},{2,18},{3,19},{4,0},{5,1},{6,22},{7,23},{8,12},{9,13},... | collective-permute-start | bytes 688136 | tf_op jit(solution)/shard_map/ppermute | solution.py:88
  16.9 8.5 %collective-permute-start.2 = (bf16[4,448,128]{2,1,0:T(8,128)(2,1)S(1)}, bf16[4,448,128]{2,1,0:T(8,128)(2,1)S(1)}, u32[]{:S(2)}, u32[]{:S(2)}) collective-permute-start(bf16[4,448,128]{2,1,0:T(8,128)(2,1)S(1)} %pad_maximum_fusion.1), channel_id=1, source_target_pairs={{0,8},{1,9},{2,3},{3,2},{4,12},{5,13},{6,7},{7,6},{8,0},{9,1},{10,... | collective-permute-start | bytes 1376264 | tf_op jit(solution)/shard_map/ppermute | solution.py:88
  25.5 16.1 %copy-start.1 = (bf16[8,448,128]{2,1,0:T(8,128)(2,1)}, bf16[8,448,128]{2,1,0:T(8,128)(2,1)S(1)}, u32[]{:S(2)}) copy-start(bf16[8,448,128]{2,1,0:T(8,128)(2,1)S(1)} %pad_maximum_fusion.refs_0_) | copy-start | bytes 2752516
  25.5 13.5 %collective-permute-start.3 = (bf16[8,448,128]{2,1,0:T(8,128)(2,1)S(1)}, bf16[8,448,128]{2,1,0:T(8,128)(2,1)S(1)}, u32[]{:S(2)}, u32[]{:S(2)}) collective-permute-start(bf16[8,448,128]{2,1,0:T(8,128)(2,1)S(1)} %pad_maximum_fusion.refs_0_), channel_id=1, source_target_pairs={{0,1},{1,0},{2,10},{3,11},{4,5},{5,4},{6,14},{7,15},{8,9},{9,8},{1... | collective-permute-start | bytes 2752520 | tf_op jit(solution)/shard_map/ppermute | solution.py:90
  27.6 12.6 %collective-permute-start.4 = (bf16[8,448,128]{2,1,0:T(8,128)(2,1)S(1)}, bf16[8,448,128]{2,1,0:T(8,128)(2,1)S(1)}, u32[]{:S(2)}, u32[]{:S(2)}) collective-permute-start(bf16[8,448,128]{2,1,0:T(8,128)(2,1)S(1)} %pad_maximum_fusion.refs_0_), channel_id=1, source_target_pairs={{0,2},{1,3},{2,0},{3,1},{4,6},{5,7},{6,4},{7,5},{8,10},{9,11},{10,... | collective-permute-start | bytes 2752520 | tf_op jit(solution)/shard_map/ppermute | solution.py:89
  39.0 2.6 %copy-start.2 = (bf16[8,448,128]{2,1,0:T(8,128)(2,1)}, bf16[8,448,128]{2,1,0:T(8,128)(2,1)S(1)}, u32[]{:S(2)}) copy-start(bf16[8,448,128]{2,1,0:T(8,128)(2,1)S(1)} %collective-permute-done.3.refs_1_) | copy-start | bytes 2752516
  39.0 2.6 %collective-permute-start.5 = (bf16[8,448,128]{2,1,0:T(8,128)(2,1)S(1)}, bf16[8,448,128]{2,1,0:T(8,128)(2,1)}, u32[]{:S(2)}, u32[]{:S(2)}) collective-permute-start(bf16[8,448,128]{2,1,0:T(8,128)(2,1)S(1)} %collective-permute-done.3.refs_1_), channel_id=1, source_target_pairs={{0,2},{1,3},{2,0},{3,1},{4,6},{5,7},{6,4},{7,5},{8,10},{9,11},{10,... | collective-permute-start | bytes 2752520 | tf_op jit(solution)/shard_map/ppermute | solution.py:91
  40.2 1.4 copy-start.3
  117.2 41.6 %copy-start.7 = (f32[8,1536]{1,0:T(8,128)S(1)}, f32[8,1536]{1,0:T(8,128)}, u32[]{:S(2)}) copy-start(f32[8,1536]{1,0:T(8,128)} %get-tuple-element.43) | copy-start | bytes 147460
  167.3 4.0 %collective-permute-start.6 = (bf16[16,448,128]{2,1,0:T(8,128)(2,1)}, bf16[16,448,128]{2,1,0:T(8,128)(2,1)S(1)}, u32[]{:S(2)}, u32[]{:S(2)}) collective-permute-start(bf16[16,448,128]{2,1,0:T(8,128)(2,1)} %get-tuple-element.45), channel_id=1, source_target_pairs={{0,2},{1,3},{2,0},{3,1},{4,6},{5,7},{6,4},{7,5},{8,10},{9,11},{10,... | collective-permute-start | bytes 5505032 | tf_op jit(solution)/shard_map/ppermute | solution.py:96
  171.3 15.3 %copy-start = (f32[16,448,128]{2,1,0:T(8,128)S(1)}, f32[16,448,128]{2,1,0:T(8,128)}, u32[]{:S(2)}) copy-start(f32[16,448,128]{2,1,0:T(8,128)} %get-tuple-element.44) | copy-start | bytes 11010052
  173.1 13.5 %collective-permute-start.7 = (bf16[8,448,128]{2,1,0:T(8,128)(2,1)S(1)}, bf16[8,448,128]{2,1,0:T(8,128)(2,1)S(1)}, u32[]{:S(2)}, u32[]{:S(2)}) collective-permute-start(bf16[8,448,128]{2,1,0:T(8,128)(2,1)S(1)} %add_convert_fusion), channel_id=1, source_target_pairs={{0,1},{1,0},{2,10},{3,11},{4,5},{5,4},{6,14},{7,15},{8,9},{9,8},{1... | collective-permute-start | bytes 2752520 | tf_op jit(solution)/shard_map/ppermute | solution.py:101
  186.8 21.9 %copy-start.4 = (f32[55416]{0:T(1024)S(1)}, f32[55416]{0:T(1024)}, u32[]{:S(2)}) copy-start(f32[55416]{0:T(1024)} %param.12) | copy-start | bytes 664996
  186.8 21.9 %copy-start.5 = (f32[55416]{0:T(1024)S(1)}, f32[55416]{0:T(1024)}, u32[]{:S(2)}) copy-start(f32[55416]{0:T(1024)} %param.14) | copy-start | bytes 664996
  186.8 21.9 %copy-start.6 = (f32[55416]{0:T(1024)S(1)}, f32[55416]{0:T(1024)}, u32[]{:S(2)}) copy-start(f32[55416]{0:T(1024)} %param.13) | copy-start | bytes 664996
  186.8 8.5 %collective-permute-start.8 = (bf16[4,448,128]{2,1,0:T(8,128)(2,1)S(1)}, bf16[4,448,128]{2,1,0:T(8,128)(2,1)S(1)}, u32[]{:S(2)}, u32[]{:S(2)}) collective-permute-start(bf16[4,448,128]{2,1,0:T(8,128)(2,1)S(1)} %add_convert_fusion.1), channel_id=1, source_target_pairs={{0,8},{1,9},{2,3},{3,2},{4,12},{5,13},{6,7},{7,6},{8,0},{9,1},{10,... | collective-permute-start | bytes 1376264 | tf_op jit(solution)/shard_map/ppermute | solution.py:101
  195.5 6.1 %collective-permute-start.9 = (bf16[2,448,128]{2,1,0:T(8,128)(2,1)S(1)}, bf16[2,448,128]{2,1,0:T(8,128)(2,1)S(1)}, u32[]{:S(2)}, u32[]{:S(2)}) collective-permute-start(bf16[2,448,128]{2,1,0:T(8,128)(2,1)S(1)} %add_convert_fusion.2), channel_id=1, source_target_pairs={{0,4},{1,5},{2,18},{3,19},{4,0},{5,1},{6,22},{7,23},{8,12},{9,13},... | collective-permute-start | bytes 688136 | tf_op jit(solution)/shard_map/ppermute | solution.py:101
  201.6 7.0 %collective-permute-start.10 = (bf16[1,448,128]{2,1,0:T(8,128)(2,1)S(1)}, bf16[1,448,128]{2,1,0:T(8,128)(2,1)S(1)}, u32[]{:S(2)}, u32[]{:S(2)}) collective-permute-start(bf16[1,448,128]{2,1,0:T(8,128)(2,1)S(1)} %add_convert_fusion.3), channel_id=1, source_target_pairs={{0,16},{1,17},{2,6},{3,7},{4,20},{5,21},{6,2},{7,3},{8,24},{9,25},... | collective-permute-start | bytes 344072 | tf_op jit(solution)/shard_map/ppermute | solution.py:101
